TPU v7x, 32 devices: a whole 2x2x4 slice. The times are simulated.
32 devices in a mesh: section: 2 (over core), dom: 16 (over z, y, x).
Axes of the slice: x: 2, y: 2, z: 4, core: 2. Of those that a mesh axis runs over, the one named last changes fastest.
Arguments:
- blocks: float32 [16, 32, 6, 128, 128], P('section', 'dom'), may hold values from -0.21875 to 0.21875
- column_index: int32 [16, 32, 6], P('section', 'dom'), may hold values from 0 to 31
- block_period: int32 [16, 32, 6], P('section', 'dom'), may hold values from 0 to 15, as said below
- cost_vector: float32 [16, 4096], P('section', 'dom'), may hold values from -6 to 6
- demand: float32 [16, 4096], P('section', 'dom'), may hold values from -12 to 12
- primal_start: float32 [16, 4096], P('section', 'dom'), may hold values from 0 to 2
- dual_start: float32 [16, 4096], P('section', 'dom'), may hold values from -3 to 3
- primal_weight: float32 [1], replicated, may hold values from 0.5 to 2
Outputs:
- primal_final: float32 [16, 4096], P('section', 'dom')
- dual_final: float32 [16, 4096], P('section', 'dom')
Inputs may be any that keep to these rules, and one draw needn't show every extreme that they name: block_period[p, r, k] is p or p - 1; it is p for k = 0 and for p = 0.
All inputs are finite; a program needn't handle non-finite values.
Results may differ from a plain program's by a relative error of at most 0.00011.
Values sent between devices are 32-bit elements; how exact they have to be, the bound alone decides.
A program may use at most 64 MiB of HBM per device.

v0:
```python
import jax
import jax.numpy as jnp
from jax import lax
from jax.sharding import PartitionSpec as P

step_scale = 0.4
epsilon = 1e-06


def passed_along(block, axis, distance):
    devices = range(lax.axis_size(axis))
    route = [(i - distance, i) for i in devices if i - distance in devices]
    return lax.ppermute(block, axis, route)


def slot_layout(column_index, block_period):
    periods_here = column_index.shape[0]
    local_period = jnp.arange(periods_here, dtype=jnp.int32)[:, None, None]
    global_period = lax.axis_index("section") * periods_here + local_period
    slot_index = local_period + block_period - global_period + 1
    return slot_index


def forward(blocks, column_index, slot_index, field):
    periods_here = field.shape[0]
    width_here = blocks.shape[-1]
    gathered = lax.all_gather(field, "dom", axis=1, tiled=True)
    carried = passed_along(gathered[-1:], "section", 1)
    stacked = jnp.concatenate([carried, gathered], axis=0)
    block_count = stacked.shape[1] // width_here
    picked = stacked.reshape(periods_here + 1, block_count, width_here)[slot_index, column_index]
    product = jnp.einsum("prkij,prkj->pri", blocks, picked, precision=lax.Precision.HIGHEST)
    return product.reshape(periods_here, -1)


def adjoint(blocks, column_index, slot_index, field):
    periods_here = field.shape[0]
    rows_here = blocks.shape[1]
    width_here = blocks.shape[-1]
    block_count = rows_here * lax.axis_size("dom")
    field_blocks = field.reshape(periods_here, rows_here, width_here)
    block_terms = jnp.einsum(
        "prkij,pri->prkj", blocks, field_blocks, precision=lax.Precision.HIGHEST
    )
    segment_ids = (slot_index * block_count + column_index).reshape(-1)
    dense_term = jax.ops.segment_sum(
        block_terms.reshape(-1, width_here),
        segment_ids,
        num_segments=(periods_here + 1) * block_count,
    )
    dense_term = dense_term.reshape(periods_here + 1, block_count * width_here)
    carried = passed_along(dense_term[:1], "section", -1)
    own_rows = dense_term[1:]
    merged = own_rows + jnp.concatenate([jnp.zeros_like(own_rows[:-1]), carried], axis=0)
    result = lax.psum_scatter(merged, "dom", scatter_dimension=1, tiled=True)
    return result


def on_device(
    blocks, column_index, block_period, cost_vector, demand, primal_start, dual_start, primal_weight
):
    slot_index = slot_layout(column_index, block_period)
    weight_now = primal_weight[0]
    tau_first = step_scale / weight_now
    sigma_first = step_scale * weight_now
    primal_one = jnp.maximum(
        0.0,
        primal_start
        - tau_first * (cost_vector - adjoint(blocks, column_index, slot_index, dual_start)),
    )
    dual_one = dual_start + sigma_first * (
        demand - forward(blocks, column_index, slot_index, 2.0 * primal_one - primal_start)
    )
    local_primal = jnp.sum((primal_one - primal_start) ** 2)
    local_dual = jnp.sum((dual_one - dual_start) ** 2)
    move_primal, move_dual = lax.psum((local_primal, local_dual), ("section", "dom"))
    weight_next = jnp.sqrt(weight_now * jnp.sqrt((move_dual + epsilon) / (move_primal + epsilon)))
    tau_second = step_scale / weight_next
    sigma_second = step_scale * weight_next
    primal_final = jnp.maximum(
        0.0,
        primal_one
        - tau_second * (cost_vector - adjoint(blocks, column_index, slot_index, dual_one)),
    )
    dual_final = dual_one + sigma_second * (
        demand - forward(blocks, column_index, slot_index, 2.0 * primal_final - primal_one)
    )
    return (primal_final, dual_final)


def solution(mesh):
    return jax.shard_map(
        on_device,
        mesh=mesh,
        in_specs=(
            P("section", "dom", None, None, None),
            P("section", "dom", None),
            P("section", "dom", None),
            P("section", "dom"),
            P("section", "dom"),
            P("section", "dom"),
            P("section", "dom"),
            P(),
        ),
        out_specs=(P("section", "dom"), P("section", "dom")),
        check_vma=False,
    )
```

profile of v0, /device:TPU:1, one launch (start us, length us, event | category | flops | bytes accessed | tf_op | source)
XLA Modules:
  0.0 288.5 jit_solution(15570511346201908841)
XLA Ops:
  7.2 0.0 copy-start.1
  7.2 0.0 copy-start.2
  7.2 0.0 reduce-scatter.3.cloned.1.call-start
  7.2 0.7 fusion.14
  8.0 0.1 copy.12
  8.1 0.1 reshape.61
  8.2 6.1 %fusion.10 = f32[8,2,1,6,128]{4,2,3,1,0:T(1,128)S(1)} fusion(f32[8,2,6,128,128]{4,3,2,1,0:T(8,128)} %param.8, f32[8,2,128,1,1]{2,0,1,3,4:T(8,128)} %bitcast.58), kind=kOutput, calls=%fused_computation.24 | convolution fusion | flops 18874368 | bytes 6348800 | tf_op jit(solution)/shard_map/prkij,pri->prkj/dot_general | solution.py:42
  14.3 0.0 copy-start
  14.3 0.0 copy-start.3
  14.3 0.9 scatter_custom_fusion
  15.2 1.9 collective-permute-start
  17.2 0.8 collective-permute-done
  18.0 0.7 pad_add_fusion.1
  18.7 0.0 reduce-scatter.3.cloned.1.call-update
  18.7 0.0 reduce-scatter.5.cloned.1.call-start
  19.4 66.6 %reduce-scatter.3.cloned.1.call-done = f32[8,256]{1,0:T(8,128)} async-done(((f32[8,4096]{1,0:T(8,128)}), f32[8,256]{1,0:T(8,128)}) %reduce-scatter.3.cloned.1.call-update) | async-done | bytes 8208 | tf_op jit(solution)/shard_map/reduce_scatter | solution.py:55
  86.0 0.0 copy-done.1
  86.1 0.0 copy-done.2
  86.1 1.3 multiply_reduce_fusion
  87.4 30.5 %all_gather.6 = f32[8,4096]{1,0:T(8,128)S(1)} all-gather(f32[8,256]{1,0:T(8,128)S(1)} %multiply_subtract_fusion.1), channel_id=1, replica_groups=mesh['section'=2,'dom'=16] {'dom'}, dimensions={1}, use_global_device_ids=true | all-gather | bytes 139264 | tf_op jit(solution)/shard_map/all_gather | solution.py:27
  117.9 1.3 collective-permute-start.1
  119.2 0.1 copy.13
  119.3 0.1 reshape.47
  119.4 19.5 %collective-permute-done.1 = f32[1,4096]{1,0:T(1,128)S(1)} collective-permute-done((f32[1,4096]{1,0:T(1,128)S(1)}, f32[1,4096]{1,0:T(1,128)S(1)}, u32[]{:S(2)}, u32[]{:S(2)}) %collective-permute-start.1) | collective-permute-done | bytes 16416 | tf_op jit(solution)/shard_map/ppermute | solution.py:13
  138.9 0.1 copy.22
  139.0 1.4 gather_fusion
  140.4 7.1 %fusion.18 = f32[8,2,1,128,1]{3,2,4,1,0:T(1,128)S(1)} fusion(f32[8,2,6,128,1]{3,4,2,1,0:T(1,128)S(1)} %bitcast.54, f32[8,2,6,128,128]{4,3,2,1,0:T(8,128)} %param.8), kind=kOutput, calls=%fused_computation.40 | convolution fusion | flops 18874368 | bytes 6348800 | tf_op jit(solution)/shard_map/prkij,prkj->pri/dot_general | solution.py:32
  147.5 0.0 copy-done
  147.5 0.0 copy-done.3
  147.5 0.7 multiply_reduce_fusion.1
  148.2 5.1 %fusion.8 = f32[8,2,1,6,128]{4,2,3,1,0:T(1,128)S(1)} fusion(f32[8,2,6,128,128]{4,3,2,1,0:T(8,128)} %param.8, f32[8,2,128,1,1]{2,0,1,3,4:T(8,128)S(1)} %bitcast.57), kind=kOutput, calls=%fused_computation.22 | convolution fusion | flops 18874368 | bytes 6348800 | tf_op jit(solution)/shard_map/prkij,pri->prkj/dot_general | solution.py:42
  153.2 0.9 scatter_custom_fusion.1
  154.2 2.1 collective-permute-start.2
  156.3 0.8 collective-permute-done.2
  157.1 0.7 pad_add_fusion
  157.8 0.0 reduce-scatter.5.cloned.1.call-update
  157.8 37.0 %all-reduce.2 = (f32[]{:T(128)}, f32[]{:T(128)}) all-reduce(f32[]{:T(128)} %get-tuple-element.8, f32[]{:T(128)} %get-tuple-element.6), channel_id=1, replica_groups=mesh['section'=2,'dom'=16] {'section','dom'}, use_global_device_ids=true, to_apply=%region_3.0 | all-reduce | flops 2 | bytes 16 | tf_op jit(solution)/shard_map/psum | solution.py:76
  196.2 23.4 %reduce-scatter.5.cloned.1.call-done = f32[8,256]{1,0:T(8,128)} async-done(((f32[8,4096]{1,0:T(8,128)}), f32[8,256]{1,0:T(8,128)}) %reduce-scatter.5.cloned.1.call-update) | async-done | bytes 8208 | tf_op jit(solution)/shard_map/reduce_scatter | solution.py:55
  219.7 1.3 multiply_subtract_fusion
  221.0 30.5 %all_gather.7 = f32[8,4096]{1,0:T(8,128)S(1)} all-gather(f32[8,256]{1,0:T(8,128)S(1)} %get-tuple-element.4), channel_id=1, replica_groups=mesh['section'=2,'dom'=16] {'dom'}, dimensions={1}, use_global_device_ids=true | all-gather | bytes 139264 | tf_op jit(solution)/shard_map/all_gather | solution.py:27
  251.5 1.5 collective-permute-start.3
  253.0 19.5 %collective-permute-done.3 = f32[1,4096]{1,0:T(1,128)S(1)} collective-permute-done((f32[1,4096]{1,0:T(1,128)S(1)}, f32[1,4096]{1,0:T(1,128)S(1)}, u32[]{:S(2)}, u32[]{:S(2)}) %collective-permute-start.3) | collective-permute-done | bytes 16416 | tf_op jit(solution)/shard_map/ppermute | solution.py:13
  272.5 0.1 copy.23
  272.5 1.4 gather_fusion.1
  273.9 7.1 %fusion.19 = f32[8,2,1,128,1]{3,2,4,1,0:T(1,128)S(1)} fusion(f32[8,2,6,128,1]{3,4,2,1,0:T(1,128)S(1)} %bitcast.53, f32[8,2,6,128,128]{4,3,2,1,0:T(8,128)} %param.8), kind=kOutput, calls=%fused_computation.41 | convolution fusion | flops 18874368 | bytes 6348800 | tf_op jit(solution)/shard_map/prkij,prkj->pri/dot_general | solution.py:32
  281.0 0.6 fusion.5
  (18 shorter events, 0.2 us)
Async XLA Ops:
  7.2 78.9 %copy-start.1 = (f32[8,256]{1,0:T(8,128)S(1)}, f32[8,256]{1,0:T(8,128)}, u32[]{:S(2)}) copy-start(f32[8,256]{1,0:T(8,128)} %param.13) | copy-start | bytes 24580
  7.2 78.9 %copy-start.2 = (f32[8,256]{1,0:T(8,128)S(1)}, f32[8,256]{1,0:T(8,128)}, u32[]{:S(2)}) copy-start(f32[8,256]{1,0:T(8,128)} %param.11) | copy-start | bytes 24580
  7.2 78.9 %reduce-scatter.3.cloned.1.call-start = ((), (), s32[]{:S(2)}) async-start(), calls=%async_computation.2 | async-start | bytes 139264 | tf_op jit(solution)/shard_map/reduce_scatter | solution.py:55
  14.3 133.2 %copy-start = (f32[8,256]{1,0:T(8,128)S(1)}, f32[8,256]{1,0:T(8,128)}, u32[]{:S(2)}) copy-start(f32[8,256]{1,0:T(8,128)} %param.14) | copy-start | bytes 24580
  14.3 133.2 %copy-start.3 = (f32[8,256]{1,0:T(8,128)S(1)}, f32[8,256]{1,0:T(8,128)}, u32[]{:S(2)}) copy-start(f32[8,256]{1,0:T(8,128)} %param.12) | copy-start | bytes 24580
  15.2 2.8 collective-permute-start
  18.7 201.0 %reduce-scatter.5.cloned.1.call-start = ((), (), s32[]{:S(2)}) async-start(), calls=%async_computation.3 | async-start | bytes 139264 | tf_op jit(solution)/shard_map/reduce_scatter | solution.py:55
  117.9 21.0 %collective-permute-start.1 = (f32[1,4096]{1,0:T(1,128)S(1)}, f32[1,4096]{1,0:T(1,128)S(1)}, u32[]{:S(2)}, u32[]{:S(2)}) collective-permute-start(f32[1,4096]{1,0:T(1,128)S(1)} %slice.46), channel_id=1, source_target_pairs={{0,16},{1,17},{2,18},{3,19},{4,20},{5,21},{6,22},{7,23},{8,24},{9,... | collective-permute-start | bytes 49160 | tf_op jit(solution)/shard_map/ppermute | solution.py:13
  154.2 2.9 %collective-permute-start.2 = (f32[1,4096]{1,0:T(1,128)S(1)}, f32[1,4096]{1,0:T(1,128)S(1)}, u32[]{:S(2)}, u32[]{:S(2)}) collective-permute-start(f32[1,4096]{1,0:T(1,128)S(1)} %bitcast.60), channel_id=1, source_target_pairs={{16,0},{17,1},{18,2},{19,3},{20,4},{21,5},{22,6},{23,7},{24,8},{25... | collective-permute-start | bytes 49160 | tf_op jit(solution)/shard_map/ppermute | solution.py:13
  251.5 21.0 %collective-permute-start.3 = (f32[1,4096]{1,0:T(1,128)S(1)}, f32[1,4096]{1,0:T(1,128)S(1)}, u32[]{:S(2)}, u32[]{:S(2)}) collective-permute-start(f32[1,4096]{1,0:T(1,128)S(1)} %slice.49), channel_id=1, source_target_pairs={{0,16},{1,17},{2,18},{3,19},{4,20},{5,21},{6,22},{7,23},{8,24},{9,... | collective-permute-start | bytes 49160 | tf_op jit(solution)/shard_map/ppermute | solution.py:13
Sparse Core Ops, SparseCore 0:
  18.8 67.1 reduce-scatter.2
  157.9 61.7 reduce-scatter.4
where the time goes:
time: 289 us; the launch traced here: 288 us
  waiting for transfers between devices  131 us (45%)
  blocking collectives  98 us (34%)
  matrix products  25.4 us (9%)
  between operations  16.4 us (6%)
  other arithmetic  7.89 us (3%)
  starting transfers between devices  6.83 us (2%)
  local copies, waits for them, and re-layouts  3.43 us (1%)
    reduce_scatter x2, waiting for transfers between devices, adjoint(): result = lax.psum_scatter(merged, 'dom', scatter_dimension=1, tiled=True)  90 us
    all_gather x2, blocking collectives, forward(): gathered = lax.all_gather(field, 'dom', axis=1, tiled=True)  61 us
    ppermute x4, waiting for transfers between devices, passed_along(): return lax.ppermute(block, axis, route)  40.5 us
    psum x1, blocking collectives, on_device(): lax.psum((local_primal, local_dual), ('section', 'dom'))  37 us
    dot_general x2, matrix products, forward(): jnp.einsum('prkij,prkj->pri', blocks, picked, precision=lax.Precision.HIG...  14.2 us
    dot_general x2, matrix products, adjoint(): jnp.einsum('prkij,pri->prkj', blocks, field_blocks, precision=lax.Precisi...  11.2 us
    ppermute x4, starting transfers between devices, passed_along(): return lax.ppermute(block, axis, route)  6.76 us
  transfers between devices with their start and end apart: 6, of which 6 were waited for; matrix products, arithmetic and copies ran while one was open for 0% of the time, Pallas kernels for 0%

commit v1 on v0

v1 whole, which is shorter than its diff:
```python
import functools

import jax
import jax.numpy as jnp
from jax import lax
from jax.experimental import pallas as pl
from jax.experimental.pallas import tpu as pltpu
from jax.sharding import PartitionSpec as P

step_scale = 0.4
epsilon = 1e-06
MESH = pl.DeviceIdType.MESH
BF = jnp.bfloat16
F32 = jnp.float32


def kernel_body(
    S, D, NP, NB, K, B,
    blocks, ci, bp, cost, demand, x0r, y0r, pw,
    xo, yo,
    bv, onehot, terms, wrow, ps, pb, ra, rb, xs, xb, g, gb, x1s, y1s, ds, dg, es, eg,
    bsem, snd, rcv_a, rcv_f, snd_d, rcv_d, snd_e, rcv_e,
):
    R = NB * NP
    TP = terms.shape[1]
    N = S * D
    me_s = lax.axis_index("section")
    me_d = lax.axis_index("dom")
    me = me_s * D + me_d
    prev_s = lax.rem(me_s + S - 1, S)
    next_s = lax.rem(me_s + 1, S)

    barrier = pltpu.get_barrier_semaphore()

    def greet(t, _):
        other = lax.rem(me + t, N)
        pl.semaphore_signal(
            barrier,
            inc=1,
            device_id={"section": lax.div(other, D), "dom": lax.rem(other, D)},
            device_id_type=MESH,
        )
        return 0

    for p in range(NP):
        pltpu.make_async_copy(blocks.at[p], bv.at[p], bsem.at[p]).start()
    lax.fori_loop(1, N, greet, 0)

    def own_rows(ref):
        return jnp.concatenate([ref[:, c * B : (c + 1) * B] for c in range(NB)], axis=0)

    lane = lax.broadcasted_iota(jnp.int32, (1, NP * TP), 1)
    target = jnp.full((1, NP * TP), -1, jnp.int32)
    for p in range(NP):
        for r in range(NB):
            for k in range(K):
                q = bp[p, r, k] - me_s * NP
                col = ci[p, r, k]
                d = lax.div(col, NB)
                c = col - d * NB
                row = jnp.where(q < 0, D * R + col, d * R + c * NP + q)
                target = jnp.where(lane == p * TP + r * K + k, row, target)
    M = onehot.shape[0]
    rows_m = lax.broadcasted_iota(jnp.int32, (M, NP * TP), 0)
    onehot[...] = jnp.where(rows_m == target, 1.0, 0.0).astype(BF)
    terms[...] = jnp.zeros_like(terms)

    ii = lax.broadcasted_iota(jnp.int32, (B, B), 0)
    jj = lax.broadcasted_iota(jnp.int32, (B, B), 1)
    eye = ii == jj
    riota = lax.broadcasted_iota(jnp.int32, (R, B), 0)

    def main_copy(src, dst, recv, o):
        d = lax.rem(me_d + o, D)
        return pltpu.make_async_remote_copy(
            src_ref=src(d), dst_ref=dst, send_sem=snd.at[0, o], recv_sem=recv.at[0, o],
            device_id={"section": me_s, "dom": d}, device_id_type=MESH,
        )

    def edge_copy(src, dst, recv, sec, o):
        d = lax.rem(me_d + o, D)
        return pltpu.make_async_remote_copy(
            src_ref=src(d), dst_ref=dst, send_sem=snd.at[1, o], recv_sem=recv.at[1, o],
            device_id={"section": sec, "dom": d}, device_id_type=MESH,
        )

    def loop(lo, hi, f):
        def step(o, _):
            f(o)
            return 0

        lax.fori_loop(lo, hi, step, 0)

    def my_rows(ref_at, d):
        return ref_at[pl.ds(pl.multiple_of(d * R, R), R)]

    def adjoint_terms(w, first):
        wrow[...] = w

        def period(p, _):
            if first:
                pltpu.make_async_copy(blocks.at[p], bv.at[p], bsem.at[p]).wait()
            for r in range(NB):
                wv = wrow[pl.ds(r * NP + p, 1), :]
                col = jnp.sum(
                    jnp.where(eye, jnp.broadcast_to(wv, (B, B)), 0.0), axis=1, keepdims=True
                )
                wb = jnp.broadcast_to(col, (B, B))
                for k in range(K):
                    terms[p, r * K + k : r * K + k + 1, :] = jnp.sum(
                        bv[p, r, k] * wb, axis=0, keepdims=True
                    )
            return 0

        lax.fori_loop(0, NP, period, 0)
        t = terms[...].reshape(NP * TP, B)
        hi = t.astype(BF)
        rest = t - hi.astype(F32)
        mid = rest.astype(BF)
        low = (rest - mid.astype(F32)).astype(BF)
        oh = onehot[...]
        part = (
            jnp.dot(oh, low, preferred_element_type=F32)
            + jnp.dot(oh, mid, preferred_element_type=F32)
        ) + jnp.dot(oh, hi, preferred_element_type=F32)
        ps[...] = part[: D * R]
        for d in range(D):
            pb[d] = part[D * R + d * NB : D * R + (d + 1) * NB]

    def adjoint_sends(i):
        src = lambda d: my_rows(ps.at, d)
        main = lambda o: main_copy(src, my_rows(ra.at[i].at, me_d), rcv_a.at[i], o)
        edge = lambda o: edge_copy(lambda d: pb.at[d], rb.at[i, me_d], rcv_a.at[i], prev_s, o)
        loop(1, D, lambda o: main(o).start())
        loop(0, D, lambda o: edge(o).start())
        return main, edge

    def adjoint_result(i, main, edge):
        ra[i, pl.ds(pl.multiple_of(me_d * R, R), R), :] = ps[
            pl.ds(pl.multiple_of(me_d * R, R), R), :
        ]
        loop(1, D, lambda o: main(o).wait())
        loop(0, D, lambda o: edge(o).wait())
        total = ra[i, 0:R, :]
        rim = rb[i, 0]
        for d in range(1, D):
            total = total + ra[i, d * R : (d + 1) * R, :]
            rim = rim + rb[i, d]
        for c in range(NB):
            total = total + jnp.where(
                riota == c * NP + NP - 1, jnp.broadcast_to(rim[c : c + 1], (R, B)), 0.0
            )
        return total

    def forward(i, xbar):
        xs[...] = xbar
        for c in range(NB):
            xb[c : c + 1, :] = xbar[c * NP + NP - 1 : c * NP + NP]
        main = lambda o: main_copy(lambda d: xs, my_rows(g.at[i].at, me_d), rcv_f.at[i], o)
        edge = lambda o: edge_copy(lambda d: xb, gb.at[i, me_d], rcv_f.at[i], next_s, o)
        loop(1, D, lambda o: main(o).start())
        loop(0, D, lambda o: edge(o).start())
        g[i, pl.ds(pl.multiple_of(me_d * R, R), R), :] = xbar
        loop(1, D, lambda o: main(o).wait())
        loop(0, D, lambda o: edge(o).wait())

        def period(p, y):
            for r in range(NB):
                acc = None
                for k in range(K):
                    q = bp[p, r, k] - me_s * NP
                    col = ci[p, r, k]
                    d = lax.div(col, NB)
                    c = col - d * NB
                    row = d * R + c * NP + jnp.maximum(q, 0)
                    xv = g[i, pl.ds(row, 1), :]
                    if k > 0:
                        xv = jnp.where(q < 0, gb[i, d, pl.ds(c, 1), :], xv)
                    term = bv[p, r, k] * jnp.broadcast_to(xv, (B, B))
                    acc = term if acc is None else acc + term
                y = jnp.where(jj == r * NP + p, jnp.sum(acc, axis=1, keepdims=True), y)
            return y

        y = lax.fori_loop(0, NP, period, jnp.zeros((B, B), F32))
        return y.T[:R]

    w0 = jnp.full((1, B), pw[0], F32)
    tau0 = step_scale / w0
    sigma0 = step_scale * w0

    adjoint_terms(own_rows(y0r), True)
    pl.semaphore_wait(barrier, N - 1)
    main, edge = adjoint_sends(0)
    at = adjoint_result(0, main, edge)
    x0 = own_rows(x0r)
    x1 = jnp.maximum(0.0, x0 - tau0 * (own_rows(cost) - at))
    x1s[...] = x1
    ax = forward(0, 2.0 * x1 - x0)
    y0 = own_rows(y0r)
    y1 = y0 + sigma0 * (own_rows(demand) - ax)
    y1s[...] = y1
    ds[0:1, :] = jnp.sum((x1s[...] - own_rows(x0r)) ** 2, axis=0, keepdims=True)
    ds[1:2, :] = jnp.sum((y1 - y0) ** 2, axis=0, keepdims=True)

    def dom_sum(o):
        d = lax.rem(me_d + o, D)
        return pltpu.make_async_remote_copy(
            src_ref=ds, dst_ref=dg.at[me_d], send_sem=snd_d.at[o], recv_sem=rcv_d.at[o],
            device_id={"section": me_s, "dom": d}, device_id_type=MESH,
        )

    def section_sum(o):
        s = lax.rem(me_s + o, S)
        return pltpu.make_async_remote_copy(
            src_ref=es, dst_ref=eg.at[me_s], send_sem=snd_e.at[o], recv_sem=rcv_e.at[o],
            device_id={"section": s, "dom": me_d}, device_id_type=MESH,
        )

    loop(1, D, lambda o: dom_sum(o).start())
    dg[me_d] = ds[...]
    adjoint_terms(y1, False)
    main, edge = adjoint_sends(1)
    loop(1, D, lambda o: dom_sum(o).wait())
    moved = dg[0]
    for d in range(1, D):
        moved = moved + dg[d]
    es[...] = moved
    loop(1, S, lambda o: section_sum(o).start())
    eg[me_s] = moved
    loop(1, S, lambda o: section_sum(o).wait())
    moved = eg[0]
    for s in range(1, S):
        moved = moved + eg[s]
    moved = jnp.sum(moved, axis=1, keepdims=True)
    dx = jnp.broadcast_to(moved[0:1], (1, B))
    dy = jnp.broadcast_to(moved[1:2], (1, B))
    omega = jnp.sqrt(w0 * jnp.sqrt((dy + epsilon) / (dx + epsilon)))
    tau1 = step_scale / omega
    sigma1 = step_scale * omega
    at = adjoint_result(1, main, edge)
    x1 = x1s[...]
    x2 = jnp.maximum(0.0, x1 - tau1 * (own_rows(cost) - at))
    for c in range(NB):
        xo[:, c * B : (c + 1) * B] = x2[c * NP : (c + 1) * NP]
    ax = forward(1, 2.0 * x2 - x1)
    y2 = y1s[...] + sigma1 * (own_rows(demand) - ax)
    for c in range(NB):
        yo[:, c * B : (c + 1) * B] = y2[c * NP : (c + 1) * NP]


def on_device(S, D, blocks, ci, bp, cost, demand, x0, y0, pw):
    NP, NB, K, B, _ = blocks.shape
    R = NB * NP
    TP = -(-NB * K // 8) * 8
    M = D * R + D * NB
    vmem = pl.BlockSpec(memory_space=pltpu.VMEM)
    smem = pl.BlockSpec(memory_space=pltpu.SMEM)
    hbm = pl.BlockSpec(memory_space=pl.ANY)
    V = lambda *s: pltpu.VMEM(s, F32)
    sem = lambda *s: pltpu.SemaphoreType.DMA(s)
    return pl.pallas_call(
        functools.partial(kernel_body, S, D, NP, NB, K, B),
        out_shape=(
            jax.ShapeDtypeStruct(x0.shape, F32),
            jax.ShapeDtypeStruct(y0.shape, F32),
        ),
        in_specs=[hbm, smem, smem, vmem, vmem, vmem, vmem, smem],
        out_specs=(vmem, vmem),
        scratch_shapes=[
            V(NP, NB, K, B, B),
            pltpu.VMEM((M, NP * TP), BF),
            V(NP, TP, B),
            V(R, B),
            V(D * R, B),
            V(D, NB, B),
            V(2, D * R, B),
            V(2, D, NB, B),
            V(R, B),
            V(NB, B),
            V(2, D * R, B),
            V(2, D, NB, B),
            V(R, B),
            V(R, B),
            V(2, B),
            V(D, 2, B),
            V(2, B),
            V(S, 2, B),
            sem(NP),
            sem(2, D),
            sem(2, 2, D),
            sem(2, 2, D),
            sem(D),
            sem(D),
            sem(S),
            sem(S),
        ],
        compiler_params=pltpu.CompilerParams(
            collective_id=0, has_side_effects=True, vmem_limit_bytes=48 * 1024 * 1024
        ),
    )(blocks, ci, bp, cost, demand, x0, y0, pw)


def solution(mesh):
    return jax.shard_map(
        functools.partial(on_device, mesh.shape["section"], mesh.shape["dom"]),
        mesh=mesh,
        in_specs=(
            P("section", "dom", None, None, None),
            P("section", "dom", None),
            P("section", "dom", None),
            P("section", "dom"),
            P("section", "dom"),
            P("section", "dom"),
            P("section", "dom"),
            P(),
        ),
        out_specs=(P("section", "dom"), P("section", "dom")),
        check_vma=False,
    )
```

time: 289 us -> 44.8 us (0.16)
  waiting for transfers between devices: 131 us -> 0 us
  blocking collectives: 98 us -> 0 us
  Pallas kernels: 0 us -> 37.5 us
  matrix products: 25.4 us -> 0 us
  between operations: 16.4 us -> 1.29 us
  other arithmetic: 7.89 us -> 0 us
  starting transfers between devices: 6.83 us -> 0 us
    reduce_scatter x2 -> x0, waiting for transfers between devices: 90 us -> none  [adjoint(): result = lax.psum_scatter(merged, 'dom', scatter_dimension=1, tiled=True)]
    all_gather x2 -> x0, blocking collectives: 61 us -> none  [forward(): gathered = lax.all_gather(field, 'dom', axis=1, tiled=True)]
    ppermute x4 -> x0, waiting for transfers between devices: 40.5 us -> none  [passed_along(): return lax.ppermute(block, axis, route)]
    pallas_call x0 -> x1, Pallas kernels: none -> 37.5 us  [on_device(): pl.pallas_call(functools.partial(kernel_body, S, D, NP, NB, K, B), out_sh...]
    psum x1 -> x0, blocking collectives: 37 us -> none  [on_device(): lax.psum((local_primal, local_dual), ('section', 'dom'))]
    dot_general x4 -> x0, matrix products: 25.4 us -> none  [the longest x2 14.2 us: forward(): jnp.einsum('prkij,prkj->pri', blocks, picked, precision=lax.Precision.HIG...]
    ppermute x4 -> x0, starting transfers between devices: 6.76 us -> none  [passed_along(): return lax.ppermute(block, axis, route)]
    unnamed x10 -> x12, local copies, waits for them, and re-layouts: 0.12 us -> 5.54 us
  transfers between devices with their start and end apart: 6 -> 0, of which waited for: 6 -> 0; matrix products, arithmetic and copies ran while one was open for 0% -> 0% of each run, Pallas kernels for 0% -> 0%
where the time goes in v1:
time: 44.8 us; the launch traced here: 44.3 us
  Pallas kernels  37.5 us (84%)
  local copies, waits for them, and re-layouts  5.54 us (12%)
  between operations  1.29 us (3%)
    pallas_call x1, Pallas kernels, on_device(): pl.pallas_call(functools.partial(kernel_body, S, D, NP, NB, K, B), out_sh...  37.5 us
    unnamed x12, local copies, waits for them, and re-layouts  5.54 us

profile of v1, /device:TPU:1, one launch (start us, length us, event | category | flops | bytes accessed | tf_op | source)
XLA Modules:
  0.0 44.3 jit_solution(9584153455141824449)
XLA Ops:
  1.3 0.8 %copy.10.ci = s32[8,2,6]{2,1,0:T(2,128)S(1)} copy(s32[8,2,6]{0,1,2:T(2,128)} %param.9) | data formatting | bytes 768 | tf_op args[1]
  2.1 0.8 %copy.11.bp = s32[8,2,6]{2,1,0:T(2,128)S(1)} copy(s32[8,2,6]{0,1,2:T(2,128)} %param.10) | data formatting | bytes 768 | tf_op args[2]
  2.8 0.0 copy-start
  2.8 0.7 %copy-done = f32[8,256]{1,0:T(8,128)S(1)} copy-done((f32[8,256]{1,0:T(8,128)S(1)}, f32[8,256]{1,0:T(8,128)}, u32[]{:S(2)}) %copy-start) | copy-done | bytes 8216
  3.5 0.0 copy-start.1
  3.5 0.7 %copy-done.1 = f32[8,256]{1,0:T(8,128)S(1)} copy-done((f32[8,256]{1,0:T(8,128)S(1)}, f32[8,256]{1,0:T(8,128)}, u32[]{:S(2)}) %copy-start.1) | copy-done | bytes 8216
  4.2 0.0 copy-start.2
  4.2 0.7 %copy-done.2 = f32[8,256]{1,0:T(8,128)S(1)} copy-done((f32[8,256]{1,0:T(8,128)S(1)}, f32[8,256]{1,0:T(8,128)}, u32[]{:S(2)}) %copy-start.2) | copy-done | bytes 8216
  4.9 0.0 copy-start.3
  4.9 0.7 %copy-done.3 = f32[8,256]{1,0:T(8,128)S(1)} copy-done((f32[8,256]{1,0:T(8,128)S(1)}, f32[8,256]{1,0:T(8,128)}, u32[]{:S(2)}) %copy-start.3) | copy-done | bytes 8216
  5.6 37.5 %shard_map.95 = (f32[8,256]{1,0:T(8,128)S(1)}, f32[8,256]{1,0:T(8,128)S(1)}) custom-call(f32[8,2,6,128,128]{4,3,2,1,0:T(8,128)} %blocks.1, s32[8,2,6]{2,1,0:T(2,128)S(1)} %copy.10.ci, s32[8,2,6]{2,1,0:T(2,128)S(1)} %copy.11.bp, f32[8,256]{1,0:T(8,128)S(1)} %copy-done, f32[8,256]{1,0:T(8,128)S(1)} %copy-done.1, f32[8,256]{1,0:T(8,128)S(1)} %copy-done.2, ...), custom_call_target="tpu_custom_call" | custom-call | tf_op jit(solution)/shard_map/pallas_call | solution.py:261
  43.1 0.6 %copy.15 = f32[8,256]{1,0:T(8,128)} copy(f32[8,256]{1,0:T(8,128)S(1)} %get-tuple-element.4) | data formatting | bytes 16384
  43.7 0.6 %copy.16 = f32[8,256]{1,0:T(8,128)} copy(f32[8,256]{1,0:T(8,128)S(1)} %get-tuple-element.5) | data formatting | bytes 16384
Async XLA Ops:
  2.8 0.7 %copy-start = (f32[8,256]{1,0:T(8,128)S(1)}, f32[8,256]{1,0:T(8,128)}, u32[]{:S(2)}) copy-start(f32[8,256]{1,0:T(8,128)} %cost.1) | copy-start | bytes 24580
  3.5 0.7 %copy-start.1 = (f32[8,256]{1,0:T(8,128)S(1)}, f32[8,256]{1,0:T(8,128)}, u32[]{:S(2)}) copy-start(f32[8,256]{1,0:T(8,128)} %demand.1) | copy-start | bytes 24580
  4.2 0.7 %copy-start.2 = (f32[8,256]{1,0:T(8,128)S(1)}, f32[8,256]{1,0:T(8,128)}, u32[]{:S(2)}) copy-start(f32[8,256]{1,0:T(8,128)} %x0r.1) | copy-start | bytes 24580
  4.9 0.7 %copy-start.3 = (f32[8,256]{1,0:T(8,128)S(1)}, f32[8,256]{1,0:T(8,128)}, u32[]{:S(2)}) copy-start(f32[8,256]{1,0:T(8,128)} %y0r.1) | copy-start | bytes 24580

commit v2 on v1

--- a/solution.py
+++ b/solution.py
@@ -16,8 +16,9 @@
 
 def kernel_body(
     S, D, NP, NB, K, B,
-    blocks, ci, bp, cost, demand, x0r, y0r, pw,
+    blocks, ci_in, bp_in, cost_in, demand_in, x0_in, y0_in, pw,
     xo, yo,
+    ci, bp, cost, demand, x0r, y0r, isem,
     bv, onehot, terms, wrow, ps, pb, ra, rb, xs, xb, g, gb, x1s, y1s, ds, dg, es, eg,
     bsem, snd, rcv_a, rcv_f, snd_d, rcv_d, snd_e, rcv_e,
 ):
@@ -42,9 +43,22 @@
         )
         return 0
 
+    staged = [
+        pltpu.make_async_copy(a, b, isem.at[i])
+        for i, (a, b) in enumerate(
+            ((y0_in, y0r), (ci_in, ci), (bp_in, bp), (cost_in, cost), (x0_in, x0r), (demand_in, demand))
+        )
+    ]
+    for c in staged[:3]:
+        c.start()
     for p in range(NP):
         pltpu.make_async_copy(blocks.at[p], bv.at[p], bsem.at[p]).start()
+    for c in staged[3:]:
+        c.start()
     lax.fori_loop(1, N, greet, 0)
+
+    for c in staged[:3]:
+        c.wait()
 
     def own_rows(ref):
         return jnp.concatenate([ref[:, c * B : (c + 1) * B] for c in range(NB)], axis=0)
@@ -54,8 +68,8 @@
     for p in range(NP):
         for r in range(NB):
             for k in range(K):
-                q = bp[p, r, k] - me_s * NP
-                col = ci[p, r, k]
+                q = bp[k, r, p] - me_s * NP
+                col = ci[k, r, p]
                 d = lax.div(col, NB)
                 c = col - d * NB
                 row = jnp.where(q < 0, D * R + col, d * R + c * NP + q)
@@ -112,7 +126,7 @@
                     )
             return 0
 
-        lax.fori_loop(0, NP, period, 0)
+        lax.fori_loop(0, NP, period, 0, unroll=8)
         t = terms[...].reshape(NP * TP, B)
         hi = t.astype(BF)
         rest = t - hi.astype(F32)
@@ -168,8 +182,8 @@
             for r in range(NB):
                 acc = None
                 for k in range(K):
-                    q = bp[p, r, k] - me_s * NP
-                    col = ci[p, r, k]
+                    q = bp[k, r, p] - me_s * NP
+                    col = ci[k, r, p]
                     d = lax.div(col, NB)
                     c = col - d * NB
                     row = d * R + c * NP + jnp.maximum(q, 0)
@@ -181,7 +195,7 @@
                 y = jnp.where(jj == r * NP + p, jnp.sum(acc, axis=1, keepdims=True), y)
             return y
 
-        y = lax.fori_loop(0, NP, period, jnp.zeros((B, B), F32))
+        y = lax.fori_loop(0, NP, period, jnp.zeros((B, B), F32), unroll=8)
         return y.T[:R]
 
     w0 = jnp.full((1, B), pw[0], F32)
@@ -189,6 +203,8 @@
     sigma0 = step_scale * w0
 
     adjoint_terms(own_rows(y0r), True)
+    for c in staged[3:]:
+        c.wait()
     pl.semaphore_wait(barrier, N - 1)
     main, edge = adjoint_sends(0)
     at = adjoint_result(0, main, edge)
@@ -264,9 +280,16 @@
             jax.ShapeDtypeStruct(x0.shape, F32),
             jax.ShapeDtypeStruct(y0.shape, F32),
         ),
-        in_specs=[hbm, smem, smem, vmem, vmem, vmem, vmem, smem],
+        in_specs=[hbm, hbm, hbm, hbm, hbm, hbm, hbm, smem],
         out_specs=(vmem, vmem),
         scratch_shapes=[
+            pltpu.SMEM((K, NB, NP), jnp.int32),
+            pltpu.SMEM((K, NB, NP), jnp.int32),
+            V(*cost.shape),
+            V(*cost.shape),
+            V(*cost.shape),
+            V(*cost.shape),
+            sem(6),
             V(NP, NB, K, B, B),
             pltpu.VMEM((M, NP * TP), BF),
             V(NP, TP, B),
@@ -297,7 +320,10 @@
         compiler_params=pltpu.CompilerParams(
             collective_id=0, has_side_effects=True, vmem_limit_bytes=48 * 1024 * 1024
         ),
-    )(blocks, ci, bp, cost, demand, x0, y0, pw)
+    )(*[
+        pltpu.with_memory_space_constraint(v, pltpu.HBM)
+        for v in (blocks, ci.transpose(2, 1, 0), bp.transpose(2, 1, 0), cost, demand, x0, y0)
+    ], pw)
 
 
 def solution(mesh):

time: 44.8 us -> 37.7 us (0.84)
  local copies, waits for them, and re-layouts: 5.54 us -> 1.2 us
  Pallas kernels: 37.5 us -> 35.1 us
    unnamed x12 -> x2, local copies, waits for them, and re-layouts: 5.54 us -> 1.2 us
    pallas_call x1, Pallas kernels: 37.5 us -> 35.1 us  [on_device(): pl.pallas_call(functools.partial(kernel_body, S, D, NP, NB, K, B), out_sh...]
where the time goes in v2:
time: 37.7 us; the launch traced here: 37.6 us
  Pallas kernels  35.1 us (93%)
  between operations  1.29 us (3%)
  local copies, waits for them, and re-layouts  1.2 us (3%)
    pallas_call x1, Pallas kernels, on_device(): pl.pallas_call(functools.partial(kernel_body, S, D, NP, NB, K, B), out_sh...  35.1 us
    unnamed x2, local copies, waits for them, and re-layouts  1.2 us

profile of v2, /device:TPU:1, one launch (start us, length us, event | category | flops | bytes accessed | tf_op | source)
XLA Modules:
  0.0 37.6 jit_solution(9448692178499074147)
XLA Ops:
  1.3 35.1 %shard_map.95 = (f32[8,256]{1,0:T(8,128)S(1)}, f32[8,256]{1,0:T(8,128)S(1)}) custom-call(f32[8,2,6,128,128]{4,3,2,1,0:T(8,128)} %blocks.1, s32[6,2,8]{2,1,0:T(2,128)} %bitcast.2, s32[6,2,8]{2,1,0:T(2,128)} %bitcast.3, f32[8,256]{1,0:T(8,128)} %cost_in.1, f32[8,256]{1,0:T(8,128)} %demand_in.1, f32[8,256]{1,0:T(8,128)} %x0_in.1, f32[8,256]{1,0:T(8,128)} %y0_in.1, ...), custom_call_target="tpu_custom_call" | custom-call | tf_op jit(solution)/shard_map/pallas_call | solution.py:277
  36.4 0.6 %copy.13 = f32[8,256]{1,0:T(8,128)} copy(f32[8,256]{1,0:T(8,128)S(1)} %get-tuple-element.4) | data formatting | bytes 16384
  37.0 0.6 %copy.14 = f32[8,256]{1,0:T(8,128)} copy(f32[8,256]{1,0:T(8,128)S(1)} %get-tuple-element.5) | data formatting | bytes 16384

commit v3 on v2

--- a/solution.py
+++ b/solution.py
@@ -55,6 +55,8 @@
         pltpu.make_async_copy(blocks.at[p], bv.at[p], bsem.at[p]).start()
     for c in staged[3:]:
         c.start()
+    rb[...] = jnp.zeros_like(rb)
+    gb[...] = jnp.zeros_like(gb)
     lax.fori_loop(1, N, greet, 0)
 
     for c in staged[:3]:
@@ -103,7 +105,7 @@
             f(o)
             return 0
 
-        lax.fori_loop(lo, hi, step, 0)
+        lax.fori_loop(lo, hi, step, 0, unroll=True)
 
     def my_rows(ref_at, d):
         return ref_at[pl.ds(pl.multiple_of(d * R, R), R)]
@@ -146,7 +148,7 @@
         main = lambda o: main_copy(src, my_rows(ra.at[i].at, me_d), rcv_a.at[i], o)
         edge = lambda o: edge_copy(lambda d: pb.at[d], rb.at[i, me_d], rcv_a.at[i], prev_s, o)
         loop(1, D, lambda o: main(o).start())
-        loop(0, D, lambda o: edge(o).start())
+        pl.when(me_s > 0)(lambda: loop(0, D, lambda o: edge(o).start()))
         return main, edge
 
     def adjoint_result(i, main, edge):
@@ -154,7 +156,8 @@
             pl.ds(pl.multiple_of(me_d * R, R), R), :
         ]
         loop(1, D, lambda o: main(o).wait())
-        loop(0, D, lambda o: edge(o).wait())
+        pl.when(me_s > 0)(lambda: loop(0, D, lambda o: edge(o).wait_send()))
+        pl.when(me_s < S - 1)(lambda: loop(0, D, lambda o: edge(o).wait_recv()))
         total = ra[i, 0:R, :]
         rim = rb[i, 0]
         for d in range(1, D):
@@ -173,10 +176,11 @@
         main = lambda o: main_copy(lambda d: xs, my_rows(g.at[i].at, me_d), rcv_f.at[i], o)
         edge = lambda o: edge_copy(lambda d: xb, gb.at[i, me_d], rcv_f.at[i], next_s, o)
         loop(1, D, lambda o: main(o).start())
-        loop(0, D, lambda o: edge(o).start())
+        pl.when(me_s < S - 1)(lambda: loop(0, D, lambda o: edge(o).start()))
         g[i, pl.ds(pl.multiple_of(me_d * R, R), R), :] = xbar
         loop(1, D, lambda o: main(o).wait())
-        loop(0, D, lambda o: edge(o).wait())
+        pl.when(me_s < S - 1)(lambda: loop(0, D, lambda o: edge(o).wait_send()))
+        pl.when(me_s > 0)(lambda: loop(0, D, lambda o: edge(o).wait_recv()))
 
         def period(p, y):
             for r in range(NB):

time: 37.7 us -> 36.8 us (0.976)
  Pallas kernels: 35.1 us -> 34.1 us
    pallas_call x1, Pallas kernels: 35.1 us -> 34.1 us  [on_device(): pl.pallas_call(functools.partial(kernel_body, S, D, NP, NB, K, B), out_sh...]
where the time goes in v3:
time: 36.8 us; the launch traced here: 36.6 us
  Pallas kernels  34.1 us (93%)
  between operations  1.29 us (4%)
  local copies, waits for them, and re-layouts  1.2 us (3%)
    pallas_call x1, Pallas kernels, on_device(): pl.pallas_call(functools.partial(kernel_body, S, D, NP, NB, K, B), out_sh...  34.1 us
    unnamed x2, local copies, waits for them, and re-layouts  1.2 us

profile of v3, /device:TPU:1, one launch (start us, length us, event | category | flops | bytes accessed | tf_op | source)
XLA Modules:
  0.0 36.6 jit_solution(15281988773700065126)
XLA Ops:
  1.3 34.1 %shard_map.95 = (f32[8,256]{1,0:T(8,128)S(1)}, f32[8,256]{1,0:T(8,128)S(1)}) custom-call(f32[8,2,6,128,128]{4,3,2,1,0:T(8,128)} %blocks.1, s32[6,2,8]{2,1,0:T(2,128)} %bitcast.2, s32[6,2,8]{2,1,0:T(2,128)} %bitcast.3, f32[8,256]{1,0:T(8,128)} %cost_in.1, f32[8,256]{1,0:T(8,128)} %demand_in.1, f32[8,256]{1,0:T(8,128)} %x0_in.1, f32[8,256]{1,0:T(8,128)} %y0_in.1, ...), custom_call_target="tpu_custom_call" | custom-call | tf_op jit(solution)/shard_map/pallas_call | solution.py:281
  35.4 0.6 %copy.13 = f32[8,256]{1,0:T(8,128)} copy(f32[8,256]{1,0:T(8,128)S(1)} %get-tuple-element.4) | data formatting | bytes 16384
  36.0 0.6 %copy.14 = f32[8,256]{1,0:T(8,128)} copy(f32[8,256]{1,0:T(8,128)S(1)} %get-tuple-element.5) | data formatting | bytes 16384
